TPU v7x, 32 devices: a whole 2x2x4 slice. The times are simulated.
32 devices in a mesh: dp: 8 (over y, x, core), mp: 4 (over z).
Axes of the slice: x: 2, y: 2, z: 4, core: 2. Of those that a mesh axis runs over, the one named last changes fastest.
Arguments:
- hidden_in: bfloat16 [16384, 2048], P('dp', 'mp')
- positions: int32 [16384], P('dp'), may hold values from 0 to 1023, as said below
- head_counts: int32 [4], replicated, may hold values from 4 to 6, as said below
- attention_gain: float32 [2048], P('mp'), may hold values from 0.5 to 1.5
- query_projection_weight: bfloat16 [2048, 1536], P(None, 'mp'), may hold values from -0.125 to 0.125
- key_weight: bfloat16 [2048, 320], replicated, may hold values from -0.125 to 0.125
- value_weight: bfloat16 [2048, 320], replicated, may hold values from -0.125 to 0.125
- query_gain: float32 [64], replicated, may hold values from 0.25 to 1.75
- key_gain: float32 [64], replicated, may hold values from 0.25 to 1.75
- output_weight: bfloat16 [1536, 2048], P(None, 'mp'), may hold values from -0.75 to 0.75
- feedforward_gain: float32 [2048], P('mp'), may hold values from 0.5 to 1.5
- gate_weight: bfloat16 [2048, 4096], P(None, 'mp'), may hold values from -0.125 to 0.125
- up_weight: bfloat16 [2048, 4096], P(None, 'mp'), may hold values from -0.125 to 0.125
- down_projection_weight: bfloat16 [4096, 2048], P('mp'), may hold values from -0.125 to 0.125
- cotangent: bfloat16 [16384, 2048], P('dp', 'mp'), may hold values from -6 to 6
Outputs:
- output: bfloat16 [16384, 2048], P('dp', 'mp')
- input_gradient: float32 [16384, 2048], P('dp', 'mp')
- attention_gain_gradient: float32 [2048], P('mp')
- query_weight_gradient: float32 [2048, 1536], P(None, 'mp')
- key_weight_gradient: float32 [2048, 320], replicated
- value_weight_gradient: float32 [2048, 320], replicated
- query_gain_gradient: float32 [64], replicated
- key_gain_gradient: float32 [64], replicated
- output_projection_gradient: float32 [1536, 2048], P(None, 'mp')
- feedforward_gain_gradient: float32 [2048], P('mp')
- gate_weight_gradient: float32 [2048, 4096], P(None, 'mp')
- up_weight_gradient: float32 [2048, 4096], P(None, 'mp')
- down_weight_gradient: float32 [4096, 2048], P('mp')
Inputs may be any that keep to these rules, and one draw needn't show every extreme that they name: `head_counts`: the counts sum to 20; index m's live heads follow those of lower indices; the largest count is 6 in every draw. `positions`: position ids count up by one along each sequence of 1024 tokens and restart at zero at its start and at up to three points inside it; the first sequence of all has no restart inside it.
All inputs are finite; a program needn't handle non-finite values.
Results may differ from a plain program's by a relative error of at most 0.025.
Values may be sent and summed in bfloat16 or wider, within the bound.
No kernel may reach another device: no remote copies, remote signals or barrier semaphores. Data moves between devices by JAX's collectives and lax.ppermute only.
A program may use at most 256 MiB of HBM per device.

v0:
```python
import math
import jax
import jax.numpy as jnp
from jax import lax
from jax.sharding import PartitionSpec as P

D = 2048
QH = 20
KVH = 5
HD = 64
LEN = 1024
BLK = 512
NBLK = 2
epsilon = 1e-05
rope_base = 10000.0
masked_score = -1e30


def rotary_tables(positions):
    half = HD // 2
    inverse = jnp.exp(-math.log(rope_base) * (2.0 * jnp.arange(half, dtype=jnp.float32)) / HD)
    angles = positions.astype(jnp.float32)[..., None] * inverse
    angles = jnp.concatenate([angles, angles], axis=-1)
    return (jnp.cos(angles), jnp.sin(angles))


def rotate(vectors, cosine, sine):
    half = vectors.shape[-1] // 2
    turned = jnp.concatenate([-vectors[..., half:], vectors[..., :half]], axis=-1)
    return vectors * cosine + turned * sine


def head_norm(vectors, gain):
    return vectors * lax.rsqrt(jnp.mean(vectors * vectors, axis=-1, keepdims=True) + epsilon) * gain


def inner(left_operand, right_operand):
    return lax.dot_general(
        left_operand, right_operand, (((0,), (0,)), ((), ())), preferred_element_type=jnp.float32
    )


def against(left_operand, right_operand):
    return lax.dot_general(
        left_operand, right_operand, (((1,), (1,)), ((), ())), preferred_element_type=jnp.float32
    )


def norm_forward(values, gain):
    squares = lax.psum(jnp.sum(values * values, axis=1), "mp")
    rms = lax.rsqrt(squares / D + epsilon)[:, None]
    normed = (values * rms * gain).astype(jnp.bfloat16)
    return (rms, lax.all_gather(normed, "mp", axis=1, tiled=True))


def norm_backward(values, rms, gain, normed_grad):
    weighted = normed_grad * gain
    dotted = lax.psum(jnp.sum(weighted * values, axis=1), "mp")[:, None]
    grad = weighted * rms - values * (rms * rms * rms) * dotted / D
    gain_grad = jnp.sum(normed_grad * values * rms, axis=0)
    return (grad, gain_grad)


def spread_sum(terms):
    return lax.psum_scatter(
        terms.astype(jnp.bfloat16), "mp", scatter_dimension=1, tiled=True
    ).astype(jnp.float32)


def on_device(
    hidden_in,
    positions,
    head_counts,
    attention_gain,
    query_projection_weight,
    key_weight,
    value_weight,
    query_gain,
    key_gain,
    output_weight,
    feedforward_gain,
    gate_weight,
    up_weight,
    down_projection_weight,
    cotangent,
):
    parts = lax.axis_size("mp")
    rank = lax.axis_index("mp")
    tokens = hidden_in.shape[0]
    share = hidden_in.shape[1]
    slots_here = query_projection_weight.shape[1] // HD
    seqs = tokens // LEN
    scale = 1.0 / math.sqrt(HD)
    ranks = jnp.arange(parts, dtype=jnp.int32)
    offset = jnp.sum(jnp.where(ranks < rank, head_counts, 0))
    count = jnp.sum(jnp.where(ranks == rank, head_counts, 0))
    within = jnp.arange(slots_here, dtype=jnp.int32)
    live = (within < count).astype(jnp.float32)
    groups = jnp.minimum((offset + within) // (QH // KVH), KVH - 1)
    choose = (groups[:, None] == jnp.arange(KVH, dtype=jnp.int32)[None, :]).astype(jnp.float32)
    choose_low = choose.astype(jnp.bfloat16)
    cosine, sine = rotary_tables(positions)

    def turn(raw, gain):
        heads = raw.reshape(tokens, -1, HD)
        return rotate(head_norm(heads, gain), cosine[:, None, :], sine[:, None, :])

    inputs = hidden_in.astype(jnp.float32)
    first_rms, normed_full = norm_forward(inputs, attention_gain)
    queries = jnp.dot(normed_full, query_projection_weight, preferred_element_type=jnp.float32)
    keys = jnp.dot(normed_full, key_weight, preferred_element_type=jnp.float32)
    values_low = jnp.dot(normed_full, value_weight, preferred_element_type=jnp.float32).astype(
        jnp.bfloat16
    )
    turned_queries, query_pull = jax.vjp(turn, queries, query_gain)
    turned_keys, key_pull = jax.vjp(turn, keys, key_gain)
    turned_queries = turned_queries.astype(jnp.bfloat16)
    turned_keys = turned_keys.astype(jnp.bfloat16)
    query_heads = jnp.transpose(turned_queries.reshape(seqs, LEN, slots_here, HD), (0, 2, 1, 3))
    key_heads = jnp.einsum(
        "hg,slgd->shld",
        choose_low,
        turned_keys.reshape(seqs, LEN, KVH, HD),
        preferred_element_type=jnp.float32,
    ).astype(jnp.bfloat16)
    value_heads = jnp.einsum(
        "hg,slgd->shld",
        choose_low,
        values_low.reshape(seqs, LEN, KVH, HD),
        preferred_element_type=jnp.float32,
    ).astype(jnp.bfloat16)
    query_blocks = jnp.moveaxis(query_heads.reshape(seqs, slots_here, NBLK, BLK, HD), 2, 0)
    starts = jnp.arange(NBLK, dtype=jnp.int32) * BLK
    cols = jnp.arange(LEN, dtype=jnp.int32)

    def block_scores(block, start):
        scores = (
            jnp.einsum("shid,shjd->shij", block, key_heads, preferred_element_type=jnp.float32)
            * scale
        )
        rows = start + jnp.arange(BLK, dtype=jnp.int32)
        allowed = cols[None, :] <= rows[:, None]
        return jnp.where(allowed, scores, masked_score)

    def attend_block(block_args):
        block, start = block_args
        scores = block_scores(block, start)
        peak = jnp.max(scores, axis=-1, keepdims=True)
        weights = jnp.exp(scores - peak)
        total = jnp.sum(weights, axis=-1, keepdims=True)
        probs = (weights / total).astype(jnp.bfloat16)
        result = jnp.einsum(
            "shij,shjd->shid", probs, value_heads, preferred_element_type=jnp.float32
        )
        return (result, (peak + jnp.log(total))[..., 0])

    mixed, row_totals = lax.map(attend_block, (query_blocks, starts))
    mixed = jnp.moveaxis(mixed, 0, 2).reshape(seqs, slots_here, LEN, HD).astype(jnp.bfloat16)
    mixed = mixed * live.astype(jnp.bfloat16)[None, :, None, None]
    mixed_local = jnp.transpose(mixed, (0, 2, 1, 3)).reshape(tokens, slots_here * HD)
    all_heads = lax.all_gather(mixed_local, "mp", axis=1, tiled=True)
    branch = jnp.dot(all_heads, output_weight, preferred_element_type=jnp.float32)
    middle = inputs + branch
    second_rms, second_normed_complete = norm_forward(middle, feedforward_gain)
    gate = jnp.dot(second_normed_complete, gate_weight, preferred_element_type=jnp.float32)
    up = jnp.dot(second_normed_complete, up_weight, preferred_element_type=jnp.float32)
    sigma = jax.nn.sigmoid(gate)
    swish = gate * sigma
    hidden = (swish * up).astype(jnp.bfloat16)
    down_terms = jnp.dot(hidden, down_projection_weight, preferred_element_type=jnp.float32)
    output = (
        middle
        + lax.psum_scatter(
            down_terms.astype(jnp.bfloat16), "mp", scatter_dimension=1, tiled=True
        ).astype(jnp.float32)
    ).astype(jnp.bfloat16)
    cotangent_full = lax.all_gather(cotangent, "mp", axis=1, tiled=True)
    down_grad = inner(hidden, cotangent_full)
    hidden_grad = against(cotangent_full, down_projection_weight)
    gate_grad = (hidden_grad * up * sigma * (1.0 + gate * (1.0 - sigma))).astype(jnp.bfloat16)
    up_grad = (hidden_grad * swish).astype(jnp.bfloat16)
    gate_weight_grad = inner(second_normed_complete, gate_grad)
    up_weight_grad = inner(second_normed_complete, up_grad)
    normed_two_grad = spread_sum(against(gate_grad, gate_weight) + against(up_grad, up_weight))
    middle_part, feedforward_gain_grad = norm_backward(
        middle, second_rms, feedforward_gain, normed_two_grad
    )
    middle_grad = cotangent.astype(jnp.float32) + middle_part
    branch_grad = middle_grad.astype(jnp.bfloat16)
    output_weight_grad = inner(all_heads, branch_grad)
    slot_terms = against(branch_grad, output_weight)
    mixed_grad = lax.psum_scatter(
        slot_terms.astype(jnp.bfloat16), "mp", scatter_dimension=1, tiled=True
    ).astype(jnp.float32)
    mixed_grad = (mixed_grad.reshape(tokens, slots_here, HD) * live[None, :, None]).astype(
        jnp.bfloat16
    )
    grad_heads = jnp.transpose(mixed_grad.reshape(seqs, LEN, slots_here, HD), (0, 2, 1, 3))
    grad_blocks = jnp.moveaxis(grad_heads.reshape(seqs, slots_here, NBLK, BLK, HD), 2, 0)

    def back_block(carry, block_args):
        key_total, value_total = carry
        block, grad_block, row_total, start = block_args
        scores = block_scores(block, start)
        probs = jnp.exp(scores - row_total[..., None])
        probs_low = probs.astype(jnp.bfloat16)
        prob_grad = jnp.einsum(
            "shid,shjd->shij", grad_block, value_heads, preferred_element_type=jnp.float32
        )
        delta = jnp.sum(probs * prob_grad, axis=-1, keepdims=True)
        score_grad = (probs * (prob_grad - delta)).astype(jnp.bfloat16)
        query_grad = (
            jnp.einsum("shij,shjd->shid", score_grad, key_heads, preferred_element_type=jnp.float32)
            * scale
        )
        key_total = (
            key_total
            + jnp.einsum("shij,shid->shjd", score_grad, block, preferred_element_type=jnp.float32)
            * scale
        )
        value_total = value_total + jnp.einsum(
            "shij,shid->shjd", probs_low, grad_block, preferred_element_type=jnp.float32
        )
        return ((key_total, value_total), query_grad)

    empty = jnp.zeros((seqs, slots_here, LEN, HD), jnp.float32)
    (key_slot_grad, value_slot_grad), query_block_grads = lax.scan(
        back_block, (empty, empty), (query_blocks, grad_blocks, row_totals, starts)
    )
    query_rot_grad = jnp.moveaxis(query_block_grads, 0, 2).reshape(seqs, slots_here, LEN, HD)
    query_rot_grad = jnp.transpose(query_rot_grad, (0, 2, 1, 3)).reshape(tokens, slots_here, HD)
    key_rot_grad = jnp.einsum("hg,shld->slgd", choose, key_slot_grad).reshape(tokens, KVH, HD)
    value_grad = jnp.einsum("hg,shld->slgd", choose, value_slot_grad).reshape(tokens, KVH * HD)
    query_unrotated_gradient, query_gain_part = query_pull(query_rot_grad)
    key_raw_grad, key_gain_part = key_pull(key_rot_grad)
    summed = (
        lax.psum(key_raw_grad.astype(jnp.bfloat16), "mp").astype(jnp.float32),
        lax.psum(value_grad.astype(jnp.bfloat16), "mp").astype(jnp.float32),
        lax.psum(query_gain_part.astype(jnp.bfloat16), "mp").astype(jnp.float32),
        lax.psum(key_gain_part.astype(jnp.bfloat16), "mp").astype(jnp.float32),
    )
    keys_low = summed[0].astype(jnp.bfloat16)
    values_grad_low = summed[1].astype(jnp.bfloat16)
    queries_low = query_unrotated_gradient.astype(jnp.bfloat16)
    query_weight_grad = inner(normed_full, queries_low)
    key_weight_grad = inner(normed_full, keys_low)
    value_weight_grad = inner(normed_full, values_grad_low)
    normed_grad = spread_sum(against(queries_low, query_projection_weight))
    key_rows = lax.dynamic_slice_in_dim(key_weight, rank * share, share, 0)
    value_rows = lax.dynamic_slice_in_dim(value_weight, rank * share, share, 0)
    normed_grad = normed_grad + against(keys_low, key_rows) + against(values_grad_low, value_rows)
    input_part, attention_gain_grad = norm_backward(inputs, first_rms, attention_gain, normed_grad)
    input_gradient = middle_grad + input_part
    totals = (
        lax.psum(attention_gain_grad.astype(jnp.bfloat16), "dp").astype(jnp.float32),
        lax.psum(query_weight_grad.astype(jnp.bfloat16), "dp").astype(jnp.float32),
        lax.psum(key_weight_grad.astype(jnp.bfloat16), "dp").astype(jnp.float32),
        lax.psum(value_weight_grad.astype(jnp.bfloat16), "dp").astype(jnp.float32),
        lax.psum(summed[2].astype(jnp.bfloat16), "dp").astype(jnp.float32),
        lax.psum(summed[3].astype(jnp.bfloat16), "dp").astype(jnp.float32),
        lax.psum(output_weight_grad.astype(jnp.bfloat16), "dp").astype(jnp.float32),
        lax.psum(feedforward_gain_grad.astype(jnp.bfloat16), "dp").astype(jnp.float32),
        lax.psum(gate_weight_grad.astype(jnp.bfloat16), "dp").astype(jnp.float32),
        lax.psum(up_weight_grad.astype(jnp.bfloat16), "dp").astype(jnp.float32),
        lax.psum(down_grad.astype(jnp.bfloat16), "dp").astype(jnp.float32),
    )
    return (
        output,
        input_gradient,
        totals[0],
        totals[1],
        totals[2],
        totals[3],
        totals[4],
        totals[5],
        totals[6],
        totals[7],
        totals[8],
        totals[9],
        totals[10],
    )


def solution(mesh):
    in_specs = (
        P("dp", "mp"),
        P("dp"),
        P(),
        P("mp"),
        P(None, "mp"),
        P(),
        P(),
        P(),
        P(),
        P(None, "mp"),
        P("mp"),
        P(None, "mp"),
        P(None, "mp"),
        P("mp", None),
        P("dp", "mp"),
    )
    out_specs = (
        P("dp", "mp"),
        P("dp", "mp"),
        P("mp"),
        P(None, "mp"),
        P(),
        P(),
        P(),
        P(),
        P(None, "mp"),
        P("mp"),
        P(None, "mp"),
        P(None, "mp"),
        P("mp", None),
    )
    return jax.shard_map(
        on_device, mesh=mesh, in_specs=in_specs, out_specs=out_specs, check_vma=False
    )
```

profile of v0, /device:TPU:0, one launch (start us, length us, event | category | flops | bytes accessed | tf_op | source)
XLA Modules:
  0.0 2038.4 jit_solution(6352952060460513605)
XLA Ops:
  13.3 13.7 psum.133
  43.9 135.8 %all-gather.5.cloned.1.call-done = bf16[2048,2048]{0,1:T(8,128)(2,1)} async-done(((bf16[2048,512]{0,1:T(8,128)(2,1)}), bf16[2048,2048]{0,1:T(8,128)(2,1)}) %all-gather.5.cloned.1.call-update) | async-done | bytes 8388624 | tf_op jit(solution)/shard_map/all_gather | solution.py:53
  265.4 75.8 %while.30 = (s32[]{:T(128)}, bf16[2,2,6,512,64]{3,4,2,1,0:T(8,128)(2,1)}, f32[2,2,6,512]{3,2,1,0:T(8,128)S(1)}, s32[2]{0:T(128)S(1)}, bf16[2,2,6,512,64]{3,4,2,1...) while((s32[]{:T(128)}, ...), condition=%wide.region_8.9_spmd.clone.clone, body=%wide.region_5.8_spmd.clone.sunk.clone | while | flops 1686628864 | bytes 190279856 | solution.py:157
  267.4 12.2 fusion.187
  279.6 12.3 fusion.188
  305.2 12.2 fusion.187
  317.4 12.3 fusion.188
  347.0 113.7 %all-gather.7.cloned.1.call-done = bf16[2048,1536]{0,1:T(8,128)(2,1)} async-done(((bf16[2048,384]{0,1:T(8,128)(2,1)}), bf16[2048,1536]{0,1:T(8,128)(2,1)}) %all-gather.7.cloned.1.call-update) | async-done | bytes 6291472 | tf_op jit(solution)/shard_map/all_gather | solution.py:161
  482.3 148.5 %all-gather.9.cloned.1.call-done = bf16[2048,2048]{0,1:T(8,128)(2,1)} async-done(((bf16[2048,512]{0,1:T(8,128)(2,1)}), bf16[2048,2048]{0,1:T(8,128)(2,1)}) %all-gather.9.cloned.1.call-update) | async-done | bytes 8388624 | tf_op jit(solution)/shard_map/all_gather | solution.py:53
  630.8 14.9 fusion.109
  657.3 122.8 %all-gather.11.cloned.1.call-done = bf16[2048,2048]{1,0:T(8,128)(2,1)} async-done(((bf16[2048,512]{1,0:T(8,128)(2,1)}), bf16[2048,2048]{1,0:T(8,128)(2,1)}) %all-gather.11.cloned.1.call-update) | async-done | bytes 8388624 | tf_op jit(solution)/shard_map/all_gather | solution.py:177
  780.1 23.6 %multiply_convert_fusion.1 = (bf16[2048,1024]{1,0:T(8,128)(2,1)}, bf16[2048,1024]{1,0:T(8,128)(2,1)}, bf16[2048,1024]{1,0:T(8,128)(2,1)}) fusion(f32[2048,1024]{1,0:T(8,128)} %fusion.108, f32[2048,1024]{1,0:T(8,128)} %fusion.109, bf16[2048,2048]{1,0:T(8,128)(2,1)} %all-gather.11.cloned.1.call-done, bf16[1024,2048]{1,0:T(8,128)(2,1)} %param.32), kind=kOutput, calls=%fused_computation.53 | convolution fusion | flops 8621391872 | bytes 41943040 | tf_op jit(solution)/shard_map/dot_general | solution.py:44
  803.8 15.4 fusion.110
  819.2 14.4 add_convert_fusion
  833.6 14.0 convolution_convert_fusion.2
  851.6 124.8 %reduce-scatter.9.cloned.1.call-done = bf16[2048,512]{0,1:T(8,128)(2,1)} async-done(((bf16[2048,2048]{0,1:T(8,128)(2,1)}), bf16[2048,512]{0,1:T(8,128)(2,1)}) %reduce-scatter.9.cloned.1.call-update) | async-done | bytes 2097168 | tf_op jit(solution)/shard_map/reduce_scatter | solution.py:65
  992.7 131.9 %reduce-scatter.7.cloned.1.call-done = bf16[2048,512]{0,1:T(8,128)(2,1)} async-done(((bf16[2048,2048]{0,1:T(8,128)(2,1)}), bf16[2048,512]{0,1:T(8,128)(2,1)}) %reduce-scatter.7.cloned.1.call-update) | async-done | bytes 2097168 | tf_op jit(solution)/shard_map/reduce_scatter | solution.py:173
  1150.4 14.7 convolution_convert_fusion.3
  1165.1 12.8 convolution_convert_fusion.4
  1193.4 64.9 %reduce-scatter.13.cloned.1.call-done = bf16[384,2048]{1,0:T(8,128)(2,1)} async-done(((bf16[1536,2048]{1,0:T(8,128)(2,1)}), bf16[384,2048]{1,0:T(8,128)(2,1)}) %reduce-scatter.13.cloned.1.call-update) | async-done | bytes 1572880
  1280.8 164.1 %while.31 = (s32[]{:T(128)}, f32[2,6,1024,64]{2,3,1,0:T(8,128)}, f32[2,6,1024,64]{2,3,1,0:T(8,128)}, f32[2,2,6,512,64]{3,4,2,1,0:T(8,128)}, s32[2]{0:T(128)S(1)}...) while((s32[]{:T(128)}, f32[2,6,1024,64]{2,3,1,0:T(8,128)}, ...), condition=%wide.region_19.20_spmd.clone.clone, body=%wide.region_17.19_spmd.clone.sunk.clone | while | flops 4125747712 | bytes 278057216 | solution.py:227
  1294.5 13.4 select_add_fusion.7
  1307.9 18.2 multiply_reduce_fusion.10
  1326.1 17.3 multiply_convert_fusion.8
  1374.9 14.3 select_add_fusion.7
  1389.2 18.2 multiply_reduce_fusion.10
  1407.4 17.3 multiply_convert_fusion.8
  1491.8 91.7 %all-reduce.13.cloned.1.call-done = (bf16[2048,320]{0,1:T(8,128)(2,1)}, bf16[2048,320]{0,1:T(8,128)(2,1)}) async-done(((bf16[2048,320]{0,1:T(8,128)(2,1)}, bf16[2048,320]{0,1:T(8,128)(2,1)}), (bf16[2048,320]{0,1:T(8,128)(2,1)}, bf16[2048,320]{0,1:T(8,128)(2,1)})) %all-reduce.13.cloned.1.call-update) | async-done | bytes 2621456 | tf_op jit(solution)/shard_map/psum | solution.py:237
  1625.4 210.8 %all-reduce.11.cloned.1.call-done = (bf16[2048,384]{1,0:T(8,128)(2,1)}, bf16[2048,320]{0,1:T(8,128)(2,1)}, bf16[2048,320]{0,1:T(8,128)(2,1)}, bf16[1536,512]{1,0...) async-done(((bf16[2048,384]{1,0:T(8,128)(2,1)}, bf16[2048,320]{0,1:T(8,128)(2,1)}, bf16[2048,320]{0,1:T(8,128)(2,1)}, ...) | async-done | bytes 18350096 | tf_op jit(solution)/shard_map/psum | solution.py:256
  1860.1 122.8 %reduce-scatter.11.cloned.1.call-done = bf16[2048,512]{0,1:T(8,128)(2,1)} async-done(((bf16[2048,2048]{0,1:T(8,128)(2,1)}), bf16[2048,512]{0,1:T(8,128)(2,1)}) %reduce-scatter.11.cloned.1.call-update) | async-done | bytes 2097168 | tf_op jit(solution)/shard_map/reduce_scatter | solution.py:65
  1990.7 13.5 all-reduce.4
  2006.3 11.7 psum.138
  (332 shorter events, 457.5 us)
Async XLA Ops:
  7.2 218.1 %copy-start = (bf16[2048,384]{1,0:T(8,128)(2,1)S(1)}, bf16[2048,384]{1,0:T(8,128)(2,1)}, u32[]{:S(2)}) copy-start(bf16[2048,384]{1,0:T(8,128)(2,1)} %param.23) | copy-start | bytes 4718596
  7.2 21.1 %copy-start.48 = (f32[512]{0:T(512)S(1)}, f32[512]{0:T(512)}, u32[]{:S(2)}) copy-start(f32[512]{0:T(512)} %param.22) | copy-start | bytes 6148
  7.2 172.6 %all-gather.5.cloned.1.call-start = ((), (), s32[]{:S(2)}) async-start(), calls=%async_computation.4 | async-start | bytes 10485760 | tf_op jit(solution)/shard_map/all_gather | solution.py:53
  31.7 148.1 %copy-start.43 = (bf16[2048,320]{0,1:T(8,128)(2,1)S(1)}, bf16[2048,320]{0,1:T(8,128)(2,1)}, u32[]{:S(2)}) copy-start(bf16[2048,320]{0,1:T(8,128)(2,1)} %param.25) | copy-start | bytes 3932164
  31.7 429.0 %all-gather.7.cloned.1.call-start = ((), (), s32[]{:S(2)}) async-start(), calls=%async_computation.5 | async-start | bytes 7864320 | tf_op jit(solution)/shard_map/all_gather | solution.py:161
  31.9 155.3 %copy-start.58 = (f32[32]{0:T(128)}, f32[32]{0:T(128)S(1)}, u32[]{:S(2)}) copy-start(f32[32]{0:T(128)S(1)} %multiply_exponential_fusion) | copy-start | bytes 388
  33.2 189.5 %copy-start.50 = (s32[6]{0:T(128)}, s32[6]{0:T(128)S(1)}, u32[]{:S(2)}) copy-start(s32[6]{0:T(128)S(1)} %fusion.101) | copy-start | bytes 76
  42.6 173.4 %copy-start.16 = (f32[2,1024,64]{1,0,2:T(2,128)}, f32[2,1024,64]{1,0,2:T(2,128)S(1)}, u32[]{:S(2)}) copy-start(f32[2,1024,64]{1,0,2:T(2,128)S(1)} %get-tuple-element.371) | copy-start | bytes 1572868
  267.4 24.5 %copy-start.9 = (bf16[2,6,1024,64]{2,3,1,0:T(8,128)(2,1)S(1)}, bf16[2,6,1024,64]{2,3,1,0:T(8,128)(2,1)}, u32[]{:S(2)}) copy-start(bf16[2,6,1024,64]{2,3,1,0:T(8,128)(2,1)} %get-tuple-element.557) | copy-start | bytes 4718596 | tf_op jit(solution)/shard_map/while
  279.6 15.4 copy-start.2
  305.2 24.5 %copy-start.9 = (bf16[2,6,1024,64]{2,3,1,0:T(8,128)(2,1)S(1)}, bf16[2,6,1024,64]{2,3,1,0:T(8,128)(2,1)}, u32[]{:S(2)}) copy-start(bf16[2,6,1024,64]{2,3,1,0:T(8,128)(2,1)} %get-tuple-element.557) | copy-start | bytes 4718596 | tf_op jit(solution)/shard_map/while
  345.3 115.4 %copy-start.67 = (bf16[1536,512]{1,0:T(8,128)(2,1)S(1)}, bf16[1536,512]{1,0:T(8,128)(2,1)}, u32[]{:S(2)}) copy-start(bf16[1536,512]{1,0:T(8,128)(2,1)} %param.28) | copy-start | bytes 4718596
  347.0 130.8 %copy-start.47 = (f32[512]{0:T(512)S(1)}, f32[512]{0:T(512)}, u32[]{:S(2)}) copy-start(f32[512]{0:T(512)} %param.29) | copy-start | bytes 6148
  347.0 283.8 %all-gather.9.cloned.1.call-start = ((), (), s32[]{:S(2)}) async-start(), calls=%async_computation.6 | async-start | bytes 10485760 | tf_op jit(solution)/shard_map/all_gather | solution.py:53
  481.7 298.4 %all-gather.11.cloned.1.call-start = ((), (), s32[]{:S(2)}) async-start(), calls=%async_computation.8 | async-start | bytes 10485760 | tf_op jit(solution)/shard_map/all_gather | solution.py:177
  482.3 494.1 %reduce-scatter.9.cloned.1.call-start = ((), (), s32[]{:S(2)}) async-start(), calls=%async_computation.9 | async-start | bytes 10485760 | tf_op jit(solution)/shard_map/reduce_scatter | solution.py:65
  803.8 15.4 copy-start.66
  803.8 15.4 copy-start.70
  833.6 291.0 %reduce-scatter.7.cloned.1.call-start = ((), (), s32[]{:S(2)}) async-start(), calls=%async_computation.7 | async-start | bytes 10485760 | tf_op jit(solution)/shard_map/reduce_scatter | solution.py:173
  847.7 410.7 %reduce-scatter.13.cloned.1.call-start = ((), (), s32[]{:S(2)}) async-start(), calls=%async_computation.11 | async-start | bytes 7864320
  1146.7 436.8 %all-reduce.13.cloned.1.call-start = ((), (), s32[]{:S(2)}) async-start(), calls=%async_computation.13 | async-start | bytes 5242880 | tf_op jit(solution)/shard_map/psum | solution.py:237
  1150.4 27.5 %slice-start.4 = ((s8[8388608]{0:T(1024)(128)(4,1)}), s8[4194304]{0:T(1024)(128)(4,1)S(1)}, s32[]{:S(2)}) async-start(s8[8388608]{0:T(1024)(128)(4,1)} %bitcast.239), calls=%async_computation.18 | async-start | bytes 8388608
  1165.1 23.3 %slice-start.6 = ((s8[6291456]{0:T(1024)(128)(4,1)}), s8[4194304]{0:T(1024)(128)(4,1)S(1)}, s32[]{:S(2)}) async-start(s8[6291456]{0:T(1024)(128)(4,1)} %bitcast.241), calls=%async_computation.20 | async-start | bytes 8388608
  1326.1 21.8 %copy-start.6 = (bf16[2,2,6,512,64]{3,4,2,1,0:T(8,128)(2,1)S(1)}, bf16[2,2,6,512,64]{3,4,2,1,0:T(8,128)(2,1)}, u32[]{:S(2)}) copy-start(bf16[2,2,6,512,64]{3,4,2,1,0:T(8,128)(2,1)} %get-tuple-element.583) | copy-start | bytes 4718596 | tf_op jit(solution)/shard_map/while
  1407.4 21.8 %copy-start.6 = (bf16[2,2,6,512,64]{3,4,2,1,0:T(8,128)(2,1)S(1)}, bf16[2,2,6,512,64]{3,4,2,1,0:T(8,128)(2,1)}, u32[]{:S(2)}) copy-start(bf16[2,2,6,512,64]{3,4,2,1,0:T(8,128)(2,1)} %get-tuple-element.583) | copy-start | bytes 4718596 | tf_op jit(solution)/shard_map/while
  1478.3 357.9 %all-reduce.11.cloned.1.call-start = ((), (), s32[]{:S(2)}) async-start(), calls=%async_computation.12 | async-start | bytes 36700160 | tf_op jit(solution)/shard_map/psum | solution.py:256
  1598.8 384.1 %reduce-scatter.11.cloned.1.call-start = ((), (), s32[]{:S(2)}) async-start(), calls=%async_computation.10 | async-start | bytes 10485760 | tf_op jit(solution)/shard_map/reduce_scatter | solution.py:65
  1855.6 127.3 %copy-start.33 = (bf16[2048,320]{0,1:T(8,128)(2,1)S(1)}, bf16[2048,320]{0,1:T(8,128)(2,1)}, u32[]{:S(2)}) copy-start(bf16[2048,320]{0,1:T(8,128)(2,1)} %get-tuple-element.349) | copy-start | bytes 3932164
  1855.6 127.3 %copy-start.41 = (f32[2048]{0:T(1024)S(1)}, f32[2048]{0:T(1024)}, u32[]{:S(2)}) copy-start(f32[2048]{0:T(1024)} %copy-done.40) | copy-start | bytes 24580
  1855.6 127.3 %copy-start.49 = (f32[512]{0:T(512)S(1)}, f32[512]{0:T(512)}, u32[]{:S(2)}) copy-start(f32[512]{0:T(512)} %param.22) | copy-start | bytes 6148
  1860.1 130.7 %copy-start.57 = (bf16[512]{0:T(512)(128)(2,1)S(1)}, bf16[512]{0:T(512)(128)(2,1)}, u32[]{:S(2)}) copy-start(bf16[512]{0:T(512)(128)(2,1)} %get-tuple-element.291) | copy-start | bytes 3076
  1860.1 158.0 %copy-start.46 = (f32[2048]{0:T(1024)S(1)}, f32[2048]{0:T(1024)}, u32[]{:S(2)}) copy-start(f32[2048]{0:T(1024)} %get-tuple-element.373) | copy-start | bytes 24580
  (65 other events, 342.0 us)
Sparse Core Ops, SparseCore 0:
  31.9 147.8 all-gather.4
  347.1 113.5 all-gather.6
  481.8 148.9 all-gather.8
  632.2 147.8 all-gather.10
  833.7 142.6 reduce-scatter.8
  979.2 145.3 reduce-scatter.6
  1146.8 111.4 reduce-scatter.12
  1478.4 105.0 all-reduce.12
  1598.9 237.2 all-reduce.10
  1838.4 144.4 reduce-scatter.10
where the time goes:
time: 2050 us; the launch traced here: 2040 us
  waiting for transfers between devices  1270 us (62%)
  matrix products  376 us (18%)
  other arithmetic  173 us (8%)
  local copies, waits for them, and re-layouts  134 us (7%)
  blocking collectives  69.5 us (3%)
    all_gather x2, waiting for transfers between devices, norm_forward(): return (rms, lax.all_gather(normed, 'mp', axis=1, tiled=True))  284 us
    reduce_scatter x2, waiting for transfers between devices, spread_sum(): lax.psum_scatter(terms.astype(jnp.bfloat16), 'mp', scatter_dimension=1, t...  248 us
    psum x1, waiting for transfers between devices, on_device(): lax.psum(query_weight_grad.astype(jnp.bfloat16), 'dp').astype(jnp.float32)  211 us
    reduce_scatter x1, waiting for transfers between devices, on_device(): lax.psum_scatter(down_terms.astype(jnp.bfloat16), 'mp', scatter_dimension...  132 us
    all_gather x1, waiting for transfers between devices, on_device(): cotangent_full = lax.all_gather(cotangent, 'mp', axis=1, tiled=True)  123 us
    all_gather x1, waiting for transfers between devices, on_device(): all_heads = lax.all_gather(mixed_local, 'mp', axis=1, tiled=True)  114 us
    psum x1, waiting for transfers between devices, on_device(): lax.psum(key_raw_grad.astype(jnp.bfloat16), 'mp').astype(jnp.float32)  91.7 us
    dot_general x7, matrix products, against(): lax.dot_general(left_operand, right_operand, (((1,), (1,)), ((), ())), pr...  77.7 us
  transfers between devices with their start and end apart: 10, of which 10 were waited for; matrix products, arithmetic and copies ran while one was open for 8% of the time, Pallas kernels for 0%

commit v1 on v0

--- a/solution.py
+++ b/solution.py
@@ -14,6 +14,28 @@
 epsilon = 1e-05
 rope_base = 10000.0
 masked_score = -1e30
+
+
+def laid_out(blocks, dim):
+    lengths = list(blocks.shape[1:])
+    lengths[dim] *= blocks.shape[0]
+    return jnp.moveaxis(blocks, 0, dim).reshape(lengths)
+
+
+def collected_by_bits(value, axis):
+    size = lax.axis_size(axis)
+    parts = value[None]
+    for level in range(size.bit_length() - 1):
+        stride = 1 << level
+        partner_block = lax.ppermute(parts, axis, [(i, i ^ stride) for i in range(size)])
+        both = jnp.stack([parts, partner_block])
+        upper = lax.axis_index(axis) >> level & 1
+        parts = jnp.where(upper == 0, both, both[::-1]).reshape(-1, *value.shape)
+    return parts
+
+
+def doubled_up(value, axis, dim):
+    return laid_out(collected_by_bits(value, axis), dim)
 
 
 def rotary_tables(positions):
@@ -158,7 +180,7 @@
     mixed = jnp.moveaxis(mixed, 0, 2).reshape(seqs, slots_here, LEN, HD).astype(jnp.bfloat16)
     mixed = mixed * live.astype(jnp.bfloat16)[None, :, None, None]
     mixed_local = jnp.transpose(mixed, (0, 2, 1, 3)).reshape(tokens, slots_here * HD)
-    all_heads = lax.all_gather(mixed_local, "mp", axis=1, tiled=True)
+    all_heads = doubled_up(mixed_local, "mp", 1)
     branch = jnp.dot(all_heads, output_weight, preferred_element_type=jnp.float32)
     middle = inputs + branch
     second_rms, second_normed_complete = norm_forward(middle, feedforward_gain)

time: 2050 us -> 2120 us (1.034)
  waiting for transfers between devices: 1270 us -> 1330 us
    ppermute x0 -> x2, waiting for transfers between devices: none -> 171 us  [collected_by_bits(): lax.ppermute(parts, axis, [(i, i ^ stride) for i in range(size)])]
    all_gather x1 -> x0, waiting for transfers between devices: 114 us -> none  [on_device(): all_heads = lax.all_gather(mixed_local, 'mp', axis=1, tiled=True)]
    unnamed x162 -> x167, local copies, waits for them, and re-layouts: 52.8 us -> 51.2 us
    unnamed x11 -> x10, waiting for transfers between devices: 65.6 us -> 65.9 us
  transfers between devices with their start and end apart: 10 -> 11, of which waited for: 10 -> 11; matrix products, arithmetic and copies ran while one was open for 8% -> 7% of each run, Pallas kernels for 0% -> 0%
where the time goes in v1:
time: 2120 us; the launch traced here: 2110 us
  waiting for transfers between devices  1330 us (63%)
  matrix products  373 us (18%)
  other arithmetic  185 us (9%)
  local copies, waits for them, and re-layouts  140 us (7%)
  blocking collectives  69.5 us (3%)
    all_gather x2, waiting for transfers between devices, norm_forward(): return (rms, lax.all_gather(normed, 'mp', axis=1, tiled=True))  284 us
    reduce_scatter x2, waiting for transfers between devices, spread_sum(): lax.psum_scatter(terms.astype(jnp.bfloat16), 'mp', scatter_dimension=1, t...  248 us
    psum x1, waiting for transfers between devices, on_device(): lax.psum(query_weight_grad.astype(jnp.bfloat16), 'dp').astype(jnp.float32)  211 us
    ppermute x2, waiting for transfers between devices, collected_by_bits(): lax.ppermute(parts, axis, [(i, i ^ stride) for i in range(size)])  171 us
    reduce_scatter x1, waiting for transfers between devices, on_device(): lax.psum_scatter(down_terms.astype(jnp.bfloat16), 'mp', scatter_dimension...  132 us
    all_gather x1, waiting for transfers between devices, on_device(): cotangent_full = lax.all_gather(cotangent, 'mp', axis=1, tiled=True)  123 us
    psum x1, waiting for transfers between devices, on_device(): lax.psum(key_raw_grad.astype(jnp.bfloat16), 'mp').astype(jnp.float32)  91.7 us
    dot_general x7, matrix products, against(): lax.dot_general(left_operand, right_operand, (((1,), (1,)), ((), ())), pr...  77.5 us
  transfers between devices with their start and end apart: 11, of which 11 were waited for; matrix products, arithmetic and copies ran while one was open for 7% of the time, Pallas kernels for 0%

profile of v1, /device:TPU:0, one launch (start us, length us, event | category | flops | bytes accessed | tf_op | source)
XLA Modules:
  0.0 2111.0 jit_solution(4877429889131383470)
XLA Ops:
  13.4 13.7 psum.133
  44.0 135.8 %all-gather.4.cloned.1.call-done = bf16[2048,2048]{0,1:T(8,128)(2,1)} async-done(((bf16[2048,512]{0,1:T(8,128)(2,1)}), bf16[2048,2048]{0,1:T(8,128)(2,1)}) %all-gather.4.cloned.1.call-update) | async-done | bytes 8388624 | tf_op jit(solution)/shard_map/all_gather | solution.py:75
  265.5 75.5 %while.30 = (s32[]{:T(128)}, bf16[2,2,6,512,64]{3,4,2,1,0:T(8,128)(2,1)}, f32[2,2,6,512]{3,2,1,0:T(8,128)S(1)}, s32[2]{0:T(128)S(1)}, bf16[2,2,6,512,64]{3,4,2,1...) while((s32[]{:T(128)}, ...), condition=%wide.region_8.9_spmd.clone.clone, body=%wide.region_5.8_spmd.clone.sunk.clone | while | flops 1686628864 | bytes 190279856 | solution.py:179
  267.4 12.1 fusion.189
  279.5 12.3 fusion.190
  305.0 12.1 fusion.189
  317.1 12.3 fusion.190
  353.0 33.8 %collective-permute-done = bf16[1,2048,384]{1,2,0:T(8,128)(2,1)} collective-permute-done((bf16[1,2048,384]{1,2,0:T(8,128)(2,1)}, bf16[1,2048,384]{1,2,0:T(8,128)(2,1)}, u32[]{:S(2)}, u32[]{:S(2)}) %collective-permute-start) | collective-permute-done | bytes 1572896 | tf_op jit(solution)/shard_map/ppermute | solution.py:30
  393.2 137.5 %collective-permute-done.1 = bf16[2,2048,384]{1,2,0:T(8,128)(2,1)} collective-permute-done((bf16[2,2048,384]{1,2,0:T(8,128)(2,1)}, bf16[2,2048,384]{1,2,0:T(8,128)(2,1)}, u32[]{:S(2)}, u32[]{:S(2)}) %collective-permute-start.1) | collective-permute-done | bytes 3145760 | tf_op jit(solution)/shard_map/ppermute | solution.py:30
  555.2 148.3 %all-gather.6.cloned.1.call-done = bf16[2048,2048]{0,1:T(8,128)(2,1)} async-done(((bf16[2048,512]{0,1:T(8,128)(2,1)}), bf16[2048,2048]{0,1:T(8,128)(2,1)}) %all-gather.6.cloned.1.call-update) | async-done | bytes 8388624 | tf_op jit(solution)/shard_map/all_gather | solution.py:75
  703.5 14.9 fusion.111
  730.0 123.0 %all-gather.8.cloned.1.call-done = bf16[2048,2048]{1,0:T(8,128)(2,1)} async-done(((bf16[2048,512]{1,0:T(8,128)(2,1)}), bf16[2048,2048]{1,0:T(8,128)(2,1)}) %all-gather.8.cloned.1.call-update) | async-done | bytes 8388624 | tf_op jit(solution)/shard_map/all_gather | solution.py:199
  853.0 23.5 %multiply_convert_fusion.1 = (bf16[2048,1024]{1,0:T(8,128)(2,1)}, bf16[2048,1024]{1,0:T(8,128)(2,1)}, bf16[2048,1024]{1,0:T(8,128)(2,1)}) fusion(f32[2048,1024]{1,0:T(8,128)} %fusion.110, f32[2048,1024]{1,0:T(8,128)} %fusion.111, bf16[2048,2048]{1,0:T(8,128)(2,1)} %all-gather.8.cloned.1.call-done, bf16[1024,2048]{1,0:T(8,128)(2,1)} %param.32), kind=kOutput, calls=%fused_computation.54 | convolution fusion | flops 8621391872 | bytes 41943040 | tf_op jit(solution)/shard_map/dot_general | solution.py:66
  876.5 15.4 fusion.112
  891.9 14.4 add_convert_fusion
  906.4 14.0 convolution_convert_fusion.2
  924.3 124.8 %reduce-scatter.9.cloned.1.call-done = bf16[2048,512]{0,1:T(8,128)(2,1)} async-done(((bf16[2048,2048]{0,1:T(8,128)(2,1)}), bf16[2048,512]{0,1:T(8,128)(2,1)}) %reduce-scatter.9.cloned.1.call-update) | async-done | bytes 2097168 | tf_op jit(solution)/shard_map/reduce_scatter | solution.py:87
  1065.4 131.9 %reduce-scatter.7.cloned.1.call-done = bf16[2048,512]{0,1:T(8,128)(2,1)} async-done(((bf16[2048,2048]{0,1:T(8,128)(2,1)}), bf16[2048,512]{0,1:T(8,128)(2,1)}) %reduce-scatter.7.cloned.1.call-update) | async-done | bytes 2097168 | tf_op jit(solution)/shard_map/reduce_scatter | solution.py:195
  1223.0 14.5 convolution_convert_fusion.3
  1237.5 12.9 convolution_convert_fusion.4
  1265.9 65.1 %reduce-scatter.13.cloned.1.call-done = bf16[384,2048]{1,0:T(8,128)(2,1)} async-done(((bf16[1536,2048]{1,0:T(8,128)(2,1)}), bf16[384,2048]{1,0:T(8,128)(2,1)}) %reduce-scatter.13.cloned.1.call-update) | async-done | bytes 1572880
  1353.5 164.3 %while.31 = (s32[]{:T(128)}, f32[2,6,1024,64]{2,3,1,0:T(8,128)}, f32[2,6,1024,64]{2,3,1,0:T(8,128)}, f32[2,2,6,512,64]{3,4,2,1,0:T(8,128)}, s32[2]{0:T(128)S(1)}...) while((s32[]{:T(128)}, f32[2,6,1024,64]{2,3,1,0:T(8,128)}, ...), condition=%wide.region_19.20_spmd.clone.clone, body=%wide.region_17.19_spmd.clone.sunk.clone | while | flops 4125747712 | bytes 278057216 | solution.py:249
  1367.2 13.5 select_add_fusion.7
  1380.6 18.2 multiply_reduce_fusion.10
  1398.8 17.3 multiply_convert_fusion.8
  1447.6 14.5 select_add_fusion.7
  1462.1 18.2 multiply_reduce_fusion.10
  1480.3 17.3 multiply_convert_fusion.8
  1564.6 91.7 %all-reduce.13.cloned.1.call-done = (bf16[2048,320]{0,1:T(8,128)(2,1)}, bf16[2048,320]{0,1:T(8,128)(2,1)}) async-done(((bf16[2048,320]{0,1:T(8,128)(2,1)}, bf16[2048,320]{0,1:T(8,128)(2,1)}), (bf16[2048,320]{0,1:T(8,128)(2,1)}, bf16[2048,320]{0,1:T(8,128)(2,1)})) %all-reduce.13.cloned.1.call-update) | async-done | bytes 2621456 | tf_op jit(solution)/shard_map/psum | solution.py:259
  1698.2 210.8 %all-reduce.11.cloned.1.call-done = (bf16[2048,384]{1,0:T(8,128)(2,1)}, bf16[2048,320]{0,1:T(8,128)(2,1)}, bf16[2048,320]{0,1:T(8,128)(2,1)}, bf16[1536,512]{1,0...) async-done(((bf16[2048,384]{1,0:T(8,128)(2,1)}, bf16[2048,320]{0,1:T(8,128)(2,1)}, bf16[2048,320]{0,1:T(8,128)(2,1)}, ...) | async-done | bytes 18350096 | tf_op jit(solution)/shard_map/psum | solution.py:278
  1932.8 123.0 %reduce-scatter.11.cloned.1.call-done = bf16[2048,512]{0,1:T(8,128)(2,1)} async-done(((bf16[2048,2048]{0,1:T(8,128)(2,1)}), bf16[2048,512]{0,1:T(8,128)(2,1)}) %reduce-scatter.11.cloned.1.call-update) | async-done | bytes 2097168 | tf_op jit(solution)/shard_map/reduce_scatter | solution.py:87
  2063.6 13.4 all-reduce.4
  (344 shorter events, 484.7 us)
Async XLA Ops:
  7.2 218.2 %copy-start = (bf16[2048,384]{1,0:T(8,128)(2,1)S(1)}, bf16[2048,384]{1,0:T(8,128)(2,1)}, u32[]{:S(2)}) copy-start(bf16[2048,384]{1,0:T(8,128)(2,1)} %param.23) | copy-start | bytes 4718596
  7.2 21.1 copy-start.51
  7.2 172.6 %all-gather.4.cloned.1.call-start = ((), (), s32[]{:S(2)}) async-start(), calls=%async_computation.4 | async-start | bytes 10485760 | tf_op jit(solution)/shard_map/all_gather | solution.py:75
  31.7 148.1 %copy-start.46 = (bf16[2048,320]{0,1:T(8,128)(2,1)S(1)}, bf16[2048,320]{0,1:T(8,128)(2,1)}, u32[]{:S(2)}) copy-start(bf16[2048,320]{0,1:T(8,128)(2,1)} %param.25) | copy-start | bytes 3932164
  31.8 671.7 %all-gather.6.cloned.1.call-start = ((), (), s32[]{:S(2)}) async-start(), calls=%async_computation.5 | async-start | bytes 10485760 | tf_op jit(solution)/shard_map/all_gather | solution.py:75
  31.9 155.3 %copy-start.61 = (f32[32]{0:T(128)}, f32[32]{0:T(128)S(1)}, u32[]{:S(2)}) copy-start(f32[32]{0:T(128)S(1)} %multiply_exponential_fusion) | copy-start | bytes 388
  33.2 189.6 %copy-start.53 = (s32[6]{0:T(128)}, s32[6]{0:T(128)S(1)}, u32[]{:S(2)}) copy-start(s32[6]{0:T(128)S(1)} %fusion.103) | copy-start | bytes 76
  42.7 173.5 %copy-start.19 = (f32[2,1024,64]{1,0,2:T(2,128)}, f32[2,1024,64]{1,0,2:T(2,128)S(1)}, u32[]{:S(2)}) copy-start(f32[2,1024,64]{1,0,2:T(2,128)S(1)} %get-tuple-element.373) | copy-start | bytes 1572868
  267.4 24.4 %copy-start.9 = (bf16[2,6,1024,64]{2,3,1,0:T(8,128)(2,1)S(1)}, bf16[2,6,1024,64]{2,3,1,0:T(8,128)(2,1)}, u32[]{:S(2)}) copy-start(bf16[2,6,1024,64]{2,3,1,0:T(8,128)(2,1)} %get-tuple-element.559) | copy-start | bytes 4718596 | tf_op jit(solution)/shard_map/while
  279.5 15.4 copy-start.2
  305.0 24.4 %copy-start.9 = (bf16[2,6,1024,64]{2,3,1,0:T(8,128)(2,1)S(1)}, bf16[2,6,1024,64]{2,3,1,0:T(8,128)(2,1)}, u32[]{:S(2)}) copy-start(bf16[2,6,1024,64]{2,3,1,0:T(8,128)(2,1)} %get-tuple-element.559) | copy-start | bytes 4718596 | tf_op jit(solution)/shard_map/while
  317.1 15.4 copy-start.2
  350.1 36.7 %collective-permute-start = (bf16[1,2048,384]{1,2,0:T(8,128)(2,1)}, bf16[1,2048,384]{1,2,0:T(8,128)(2,1)}, u32[]{:S(2)}, u32[]{:S(2)}) collective-permute-start(bf16[1,2048,384]{1,2,0:T(8,128)(2,1)} %broadcast_in_dim_reshape.3), channel_id=1, source_target_pairs={{0,1},{1,0},{2,3},{3,2},{4,5},{5,4},{6,7},{7,6},{8,9},{9,8},{10,11... | collective-permute-start | bytes 4718600 | tf_op jit(solution)/shard_map/ppermute | solution.py:30
  392.8 137.8 %collective-permute-start.1 = (bf16[2,2048,384]{1,2,0:T(8,128)(2,1)}, bf16[2,2048,384]{1,2,0:T(8,128)(2,1)}, u32[]{:S(2)}, u32[]{:S(2)}) collective-permute-start(bf16[2,2048,384]{1,2,0:T(8,128)(2,1)} %get-tuple-element.364), channel_id=1, source_target_pairs={{0,2},{1,3},{2,0},{3,1},{4,6},{5,7},{6,4},{7,5},{8,10},{9,11},{10,... | collective-permute-start | bytes 9437192 | tf_op jit(solution)/shard_map/ppermute | solution.py:30
  554.4 298.6 %all-gather.8.cloned.1.call-start = ((), (), s32[]{:S(2)}) async-start(), calls=%async_computation.7 | async-start | bytes 10485760 | tf_op jit(solution)/shard_map/all_gather | solution.py:199
  555.1 494.0 %reduce-scatter.9.cloned.1.call-start = ((), (), s32[]{:S(2)}) async-start(), calls=%async_computation.8 | async-start | bytes 10485760 | tf_op jit(solution)/shard_map/reduce_scatter | solution.py:87
  876.5 15.4 copy-start.69
  876.5 15.4 copy-start.73
  906.3 291.0 %reduce-scatter.7.cloned.1.call-start = ((), (), s32[]{:S(2)}) async-start(), calls=%async_computation.6 | async-start | bytes 10485760 | tf_op jit(solution)/shard_map/reduce_scatter | solution.py:195
  920.4 410.7 %reduce-scatter.13.cloned.1.call-start = ((), (), s32[]{:S(2)}) async-start(), calls=%async_computation.10 | async-start | bytes 7864320
  1219.4 436.9 %all-reduce.13.cloned.1.call-start = ((), (), s32[]{:S(2)}) async-start(), calls=%async_computation.12 | async-start | bytes 5242880 | tf_op jit(solution)/shard_map/psum | solution.py:259
  1223.0 27.5 %slice-start.6 = ((s8[8388608]{0:T(1024)(128)(4,1)}), s8[4194304]{0:T(1024)(128)(4,1)S(1)}, s32[]{:S(2)}) async-start(s8[8388608]{0:T(1024)(128)(4,1)} %bitcast.251), calls=%async_computation.19 | async-start | bytes 8388608
  1237.5 23.4 %slice-start = ((s8[6291456]{0:T(1024)(128)(4,1)}), s8[4194304]{0:T(1024)(128)(4,1)S(1)}, s32[]{:S(2)}) async-start(s8[6291456]{0:T(1024)(128)(4,1)} %bitcast.233), calls=%async_computation.13 | async-start | bytes 8388608
  1398.8 21.8 %copy-start.6 = (bf16[2,2,6,512,64]{3,4,2,1,0:T(8,128)(2,1)S(1)}, bf16[2,2,6,512,64]{3,4,2,1,0:T(8,128)(2,1)}, u32[]{:S(2)}) copy-start(bf16[2,2,6,512,64]{3,4,2,1,0:T(8,128)(2,1)} %get-tuple-element.585) | copy-start | bytes 4718596 | tf_op jit(solution)/shard_map/while
  1480.3 21.8 %copy-start.6 = (bf16[2,2,6,512,64]{3,4,2,1,0:T(8,128)(2,1)S(1)}, bf16[2,2,6,512,64]{3,4,2,1,0:T(8,128)(2,1)}, u32[]{:S(2)}) copy-start(bf16[2,2,6,512,64]{3,4,2,1,0:T(8,128)(2,1)} %get-tuple-element.585) | copy-start | bytes 4718596 | tf_op jit(solution)/shard_map/while
  1551.2 357.8 %all-reduce.11.cloned.1.call-start = ((), (), s32[]{:S(2)}) async-start(), calls=%async_computation.11 | async-start | bytes 36700160 | tf_op jit(solution)/shard_map/psum | solution.py:278
  1671.5 384.3 %reduce-scatter.11.cloned.1.call-start = ((), (), s32[]{:S(2)}) async-start(), calls=%async_computation.9 | async-start | bytes 10485760 | tf_op jit(solution)/shard_map/reduce_scatter | solution.py:87
  1928.3 127.5 %copy-start.36 = (bf16[2048,320]{0,1:T(8,128)(2,1)S(1)}, bf16[2048,320]{0,1:T(8,128)(2,1)}, u32[]{:S(2)}) copy-start(bf16[2048,320]{0,1:T(8,128)(2,1)} %get-tuple-element.349) | copy-start | bytes 3932164
  1928.3 127.5 %copy-start.44 = (f32[2048]{0:T(1024)S(1)}, f32[2048]{0:T(1024)}, u32[]{:S(2)}) copy-start(f32[2048]{0:T(1024)} %copy-done.43) | copy-start | bytes 24580
  1928.3 127.5 %copy-start.52 = (f32[512]{0:T(512)S(1)}, f32[512]{0:T(512)}, u32[]{:S(2)}) copy-start(f32[512]{0:T(512)} %param.22) | copy-start | bytes 6148
  1932.8 130.8 %copy-start.60 = (bf16[512]{0:T(512)(128)(2,1)S(1)}, bf16[512]{0:T(512)(128)(2,1)}, u32[]{:S(2)}) copy-start(bf16[512]{0:T(512)(128)(2,1)} %get-tuple-element.291) | copy-start | bytes 3076
  1932.8 158.2 %copy-start.49 = (f32[2048]{0:T(1024)S(1)}, f32[2048]{0:T(1024)}, u32[]{:S(2)}) copy-start(f32[2048]{0:T(1024)} %get-tuple-element.375) | copy-start | bytes 24580
  (69 other events, 354.6 us)
Sparse Core Ops, SparseCore 0:
  31.9 147.8 all-gather.3
  554.5 148.9 all-gather.5
  705.1 147.8 all-gather.7
  906.4 142.6 reduce-scatter.8
  1051.9 145.3 reduce-scatter.6
  1219.5 111.4 reduce-scatter.12
  1551.3 104.9 all-reduce.12
  1671.7 237.2 all-reduce.10
  1911.3 144.4 reduce-scatter.10
